TPU v7x, 32 devices: a whole 2x2x4 slice. The times are simulated.
32 devices in a mesh: expert: 4 (over y, core), fsdp: 8 (over z, x).
Axes of the slice: x: 2, y: 2, z: 4, core: 2. Of those that a mesh axis runs over, the one named last changes fastest.
Arguments:
- layer_input: bfloat16 [8192, 2048], P(('expert', 'fsdp')), may hold values from -6 to 6
- expert_ids: int32 [8192, 8], P(('expert', 'fsdp')), may hold values from 0 to 15, as said below
- slot_ids: int32 [8192, 8], P(('expert', 'fsdp')), may hold values from 0 to 255, as said below
- attn_gain: float32 [2048], replicated, may hold values from 0.25 to 1.75
- qkv_weight: bfloat16 [2048, 6144], P('fsdp'), may hold values from -0.125 to 0.125
- query_gain: float32 [128], replicated, may hold values from 0.25 to 1.75
- key_gain: float32 [128], replicated, may hold values from 0.25 to 1.75
- out_weight: bfloat16 [2048, 2048], P('fsdp'), may hold values from -1 to 1
- ffn_gain: float32 [2048], replicated, may hold values from 0.25 to 1.75
- router_weight: bfloat16 [2048, 16], P('fsdp'), may hold values from -0.0625 to 0.0625
- gate_up_weight: bfloat16 [16, 2048, 2048], P('expert', 'fsdp'), may hold values from -0.125 to 0.125
- down_weight: bfloat16 [16, 1024, 2048], P('expert', 'fsdp'), may hold values from -0.75 to 0.75
- cotangent: bfloat16 [8192, 2048], P(('expert', 'fsdp')), may hold values from -6 to 6
Outputs:
- mixed_out: bfloat16 [8192, 2048], P(('expert', 'fsdp'))
- input_grad: float32 [8192, 2048], P(('expert', 'fsdp'))
- attn_gain_grad: float32 [2048], replicated
- qkv_weight_grad: float32 [2048, 6144], P('fsdp')
- query_gain_grad: float32 [128], replicated
- key_gain_grad: float32 [128], replicated
- out_weight_grad: float32 [2048, 2048], P('fsdp')
- ffn_gain_grad: float32 [2048], replicated
- router_weight_grad: float32 [2048, 16], P('fsdp')
- gate_up_grad: float32 [16, 2048, 2048], P('expert', 'fsdp')
- down_grad: float32 [16, 1024, 2048], P('expert', 'fsdp')
Inputs may be any that keep to these rules, and one draw needn't show every extreme that they name: `expert_ids`: each row names 8 different experts. Among the 256 rows of one device no expert is named more than 256 times; in every device's rows one expert is named exactly 256 times. `slot_ids`: among the rows of one device, the routes to one expert have different slots.
All inputs are finite; a program needn't handle non-finite values.
Results may differ from a plain program's by a relative error of at most 0.022.
Values may be sent and summed in bfloat16 or wider, within the bound.
No kernel may reach another device: no remote copies, remote signals or barrier semaphores. Data moves between devices by JAX's collectives and lax.ppermute only.
A program may use at most 384 MiB of HBM per device.

v0:
```python
import jax
import jax.numpy as jnp
from jax import lax
from jax.sharding import PartitionSpec as P

EPSILON = 1e-06
ROPE_BASE = 50000.0


def normalize(values):
    factor = lax.rsqrt(jnp.mean(values * values, -1, keepdims=True) + EPSILON)
    return (values * factor, factor)


def norm_back(grad_unit, unit_val, factor):
    return factor * (grad_unit - unit_val * jnp.mean(grad_unit * unit_val, -1, keepdims=True))


def tables(length, head_size):
    half_size = head_size // 2
    frequency = ROPE_BASE ** (-(jnp.arange(half_size, dtype=jnp.float32) * 2.0 / head_size))
    angles = jnp.arange(length, dtype=jnp.float32)[:, None] * frequency[None, :]
    angles = jnp.concatenate([angles, angles], 1)
    return (jnp.cos(angles)[:, None, :], jnp.sin(angles)[:, None, :])


def rotate(values, cos_table, sine_table):
    half_size = values.shape[-1] // 2
    turned = jnp.concatenate([-values[..., half_size:], values[..., :half_size]], -1)
    return values * cos_table + turned * sine_table


def rotate_back(gradient, cos_table, sine_table):
    half_size = gradient.shape[-1] // 2
    turned_grad = gradient * sine_table
    return gradient * cos_table + jnp.concatenate(
        [turned_grad[..., half_size:], -turned_grad[..., :half_size]], -1
    )


def local(
    layer_input,
    expert_ids,
    slot_ids,
    attn_gain,
    qkv_weight,
    query_gain,
    key_gain,
    out_weight,
    ffn_gain,
    router_weight,
    gate_up_weight,
    down_weight,
    cotangent,
):
    tokens, model_width = layer_input.shape
    top_count = expert_ids.shape[1]
    head_size = query_gain.shape[0]
    head_count = model_width // head_size
    experts = router_weight.shape[1]
    hidden = gate_up_weight.shape[2] // 2
    capacity = 2 * tokens * top_count // experts
    score_scale = head_size ** (-0.5)
    source = layer_input.astype(jnp.float32)
    unit_one, factor_one = normalize(source)
    normed = (unit_one * attn_gain).astype(jnp.bfloat16)
    qkv_full, out_full, router_full = (
        lax.all_gather(qkv_weight, "fsdp", axis=0, tiled=True),
        lax.all_gather(out_weight, "fsdp", axis=0, tiled=True),
        lax.all_gather(router_weight, "fsdp", axis=0, tiled=True),
    )
    projected = jnp.dot(normed, qkv_full, preferred_element_type=jnp.float32)
    queries = projected[:, :model_width].reshape(tokens, head_count, head_size)
    keys_raw = projected[:, model_width : 2 * model_width].reshape(tokens, head_count, head_size)
    values_raw = projected[:, 2 * model_width :].reshape(tokens, head_count, head_size)
    unit_query, factor_query = normalize(queries)
    unit_key, factor_key = normalize(keys_raw)
    cos_table, sine_table = tables(tokens, head_size)
    query_rot = rotate(unit_query * query_gain, cos_table, sine_table).astype(jnp.bfloat16)
    key_rot = rotate(unit_key * key_gain, cos_table, sine_table).astype(jnp.bfloat16)
    value_low = values_raw.astype(jnp.bfloat16)
    scores = (
        jnp.einsum("qhd,khd->hqk", query_rot, key_rot, preferred_element_type=jnp.float32)
        * score_scale
    )
    top_score = jnp.max(scores, -1, keepdims=True)
    weights_raw = jnp.exp(scores - top_score)
    totals = jnp.sum(weights_raw, -1, keepdims=True)
    log_total = top_score + jnp.log(totals)
    prob_low = (weights_raw / totals).astype(jnp.bfloat16)
    mixed_heads = jnp.einsum(
        "hqk,khd->qhd", prob_low, value_low, preferred_element_type=jnp.float32
    )
    mixed_low = mixed_heads.reshape(tokens, model_width).astype(jnp.bfloat16)
    residual = source + jnp.dot(mixed_low, out_full, preferred_element_type=jnp.float32)
    unit_two, factor_two = normalize(residual)
    normed_two = (unit_two * ffn_gain).astype(jnp.bfloat16)
    logits = jnp.dot(normed_two, router_full, preferred_element_type=jnp.float32)
    onehot = (expert_ids[:, :, None] == jnp.arange(experts, dtype=jnp.int32)[None, None, :]).astype(
        jnp.float32
    )
    chosen = jnp.sum(onehot * logits[:, None, :], -1)
    gate_probs = jax.nn.softmax(chosen, -1)
    slot_index = (expert_ids * capacity + slot_ids).reshape(-1)
    copies = jnp.broadcast_to(normed_two[:, None, :], (tokens, top_count, model_width)).reshape(
        tokens * top_count, model_width
    )
    outgoing = jnp.zeros((experts * capacity, model_width), jnp.bfloat16).at[slot_index].set(copies)
    arrived = lax.all_to_all(
        outgoing.reshape(experts, capacity, model_width),
        "expert",
        split_axis=0,
        concat_axis=1,
        tiled=True,
    )
    gate_up_full, down_full = (
        lax.all_gather(gate_up_weight, "fsdp", axis=1, tiled=True),
        lax.all_gather(down_weight, "fsdp", axis=1, tiled=True),
    )
    gate_up_val = jnp.einsum(
        "erd,edf->erf", arrived, gate_up_full, preferred_element_type=jnp.float32
    )
    gate_part = gate_up_val[..., :hidden]
    up_part = gate_up_val[..., hidden:]
    sigmoid_gate = jax.nn.sigmoid(gate_part)
    activated = (gate_part * sigmoid_gate * up_part).astype(jnp.bfloat16)
    expert_out = jnp.einsum(
        "erf,efd->erd", activated, down_full, preferred_element_type=jnp.float32
    ).astype(jnp.bfloat16)
    returned = lax.all_to_all(
        expert_out, "expert", split_axis=1, concat_axis=0, tiled=True
    ).reshape(experts * capacity, model_width)
    picked = returned[slot_index].reshape(tokens, top_count, model_width).astype(jnp.float32)
    moe_sum = jnp.sum(gate_probs[:, :, None] * picked, 1)
    mixed_out = (residual + moe_sum).astype(jnp.bfloat16)
    upstream = cotangent.astype(jnp.float32)
    gate_grad = jnp.sum(picked * upstream[:, None, :], -1)
    row_grad = (
        (gate_probs[:, :, None] * upstream[:, None, :])
        .astype(jnp.bfloat16)
        .reshape(tokens * top_count, model_width)
    )
    grad_out = (
        jnp.zeros((experts * capacity, model_width), jnp.bfloat16).at[slot_index].set(row_grad)
    )
    grad_arrived = lax.all_to_all(
        grad_out.reshape(experts, capacity, model_width),
        "expert",
        split_axis=0,
        concat_axis=1,
        tiled=True,
    )
    gate_up_back, down_back = (
        lax.all_gather(gate_up_weight, "fsdp", axis=1, tiled=True),
        lax.all_gather(down_weight, "fsdp", axis=1, tiled=True),
    )
    act_grad = jnp.einsum(
        "erd,efd->erf", grad_arrived, down_back, preferred_element_type=jnp.float32
    )
    down_grad_full = jnp.einsum(
        "erf,erd->efd", activated, grad_arrived, preferred_element_type=jnp.float32
    )
    gate_grad_part = act_grad * up_part * sigmoid_gate * (1.0 + gate_part * (1.0 - sigmoid_gate))
    up_grad_part = act_grad * gate_part * sigmoid_gate
    both_grad = jnp.concatenate([gate_grad_part, up_grad_part], -1).astype(jnp.bfloat16)
    gate_up_grad_full = jnp.einsum(
        "erd,erf->edf", arrived, both_grad, preferred_element_type=jnp.float32
    )
    input_rows = jnp.einsum(
        "erf,edf->erd", both_grad, gate_up_back, preferred_element_type=jnp.float32
    ).astype(jnp.bfloat16)
    rows_back = lax.all_to_all(
        input_rows, "expert", split_axis=1, concat_axis=0, tiled=True
    ).reshape(experts * capacity, model_width)
    gate_up_grad, down_grad = (
        lax.psum_scatter(
            gate_up_grad_full.astype(jnp.bfloat16), "fsdp", scatter_dimension=1, tiled=True
        ).astype(jnp.float32),
        lax.psum_scatter(
            down_grad_full.astype(jnp.bfloat16), "fsdp", scatter_dimension=1, tiled=True
        ).astype(jnp.float32),
    )
    mean_grad = jnp.sum(gate_probs * gate_grad, -1, keepdims=True)
    chosen_grad = gate_probs * (gate_grad - mean_grad)
    logit_grad = jnp.sum(onehot * chosen_grad[:, :, None], 1).astype(jnp.bfloat16)
    router_grad_full = jnp.dot(normed_two.T, logit_grad, preferred_element_type=jnp.float32)
    routed_back = jnp.sum(
        rows_back[slot_index].reshape(tokens, top_count, model_width).astype(jnp.float32), 1
    )
    normed_two_grad = routed_back + jnp.dot(
        logit_grad, router_full.T, preferred_element_type=jnp.float32
    )
    ffn_gain_part = jnp.sum(normed_two_grad * unit_two, 0)
    residual_grad = upstream + norm_back(normed_two_grad * ffn_gain, unit_two, factor_two)
    attn_grad_low = residual_grad.astype(jnp.bfloat16)
    out_grad_full = jnp.dot(mixed_low.T, attn_grad_low, preferred_element_type=jnp.float32)
    mixed_grad = jnp.dot(attn_grad_low, out_full.T, preferred_element_type=jnp.float32).astype(
        jnp.bfloat16
    )
    mixed_grad = mixed_grad.reshape(tokens, head_count, head_size)
    value_grad = jnp.einsum(
        "hqk,qhd->khd", prob_low, mixed_grad, preferred_element_type=jnp.float32
    )
    prob_grad = jnp.einsum(
        "qhd,khd->hqk", mixed_grad, value_low, preferred_element_type=jnp.float32
    )
    scores_again = (
        jnp.einsum("qhd,khd->hqk", query_rot, key_rot, preferred_element_type=jnp.float32)
        * score_scale
    )
    prob_full = jnp.exp(scores_again - log_total)
    score_grad = (
        prob_full * (prob_grad - jnp.sum(prob_full * prob_grad, -1, keepdims=True))
    ).astype(jnp.bfloat16)
    query_grad = (
        jnp.einsum("hqk,khd->qhd", score_grad, key_rot, preferred_element_type=jnp.float32)
        * score_scale
    )
    key_grad = (
        jnp.einsum("hqk,qhd->khd", score_grad, query_rot, preferred_element_type=jnp.float32)
        * score_scale
    )
    query_grad = rotate_back(query_grad, cos_table, sine_table)
    key_grad = rotate_back(key_grad, cos_table, sine_table)
    query_gain_part = jnp.sum(query_grad * unit_query, (0, 1))
    key_gain_part = jnp.sum(key_grad * unit_key, (0, 1))
    query_pre = norm_back(query_grad * query_gain, unit_query, factor_query)
    key_pre = norm_back(key_grad * key_gain, unit_key, factor_key)
    qkv_grad_low = jnp.concatenate(
        [
            query_pre.reshape(tokens, model_width),
            key_pre.reshape(tokens, model_width),
            value_grad.reshape(tokens, model_width),
        ],
        1,
    ).astype(jnp.bfloat16)
    qkv_grad_full = jnp.dot(normed.T, qkv_grad_low, preferred_element_type=jnp.float32)
    normed_grad = jnp.dot(qkv_grad_low, qkv_full.T, preferred_element_type=jnp.float32)
    attn_gain_part = jnp.sum(normed_grad * unit_one, 0)
    input_grad = residual_grad + norm_back(normed_grad * attn_gain, unit_one, factor_one)
    qkv_shard, out_shard, router_shard = (
        lax.psum_scatter(
            qkv_grad_full.astype(jnp.bfloat16), "fsdp", scatter_dimension=0, tiled=True
        ).astype(jnp.float32),
        lax.psum_scatter(
            out_grad_full.astype(jnp.bfloat16), "fsdp", scatter_dimension=0, tiled=True
        ).astype(jnp.float32),
        lax.psum_scatter(
            router_grad_full.astype(jnp.bfloat16), "fsdp", scatter_dimension=0, tiled=True
        ).astype(jnp.float32),
    )
    qkv_weight_grad, out_weight_grad, router_weight_grad = (
        lax.psum(qkv_shard.astype(jnp.bfloat16), "expert").astype(jnp.float32),
        lax.psum(out_shard.astype(jnp.bfloat16), "expert").astype(jnp.float32),
        lax.psum(router_shard.astype(jnp.bfloat16), "expert").astype(jnp.float32),
    )
    attn_gain_grad, query_gain_grad, key_gain_grad, ffn_gain_grad = lax.psum(
        (attn_gain_part, query_gain_part, key_gain_part, ffn_gain_part), ("expert", "fsdp")
    )
    return (
        mixed_out,
        input_grad,
        attn_gain_grad,
        qkv_weight_grad,
        query_gain_grad,
        key_gain_grad,
        out_weight_grad,
        ffn_gain_grad,
        router_weight_grad,
        gate_up_grad,
        down_grad,
    )


def solution(mesh):
    return jax.shard_map(
        local,
        mesh=mesh,
        in_specs=(
            P(("expert", "fsdp"), None),
            P(("expert", "fsdp"), None),
            P(("expert", "fsdp"), None),
            P(),
            P("fsdp", None),
            P(),
            P(),
            P("fsdp", None),
            P(),
            P("fsdp", None),
            P("expert", "fsdp", None),
            P("expert", "fsdp", None),
            P(("expert", "fsdp"), None),
        ),
        out_specs=(
            P(("expert", "fsdp"), None),
            P(("expert", "fsdp"), None),
            P(),
            P("fsdp", None),
            P(),
            P(),
            P("fsdp", None),
            P(),
            P("fsdp", None),
            P("expert", "fsdp", None),
            P("expert", "fsdp", None),
        ),
        check_vma=False,
    )
```

profile of v0, /device:TPU:0, one launch (start us, length us, event | category | flops | bytes accessed | tf_op | source)
XLA Modules:
  0.0 3566.4 jit_solution(18210329636455333657)
XLA Ops:
  9.7 1.5 convert_element_type.132
  11.3 67.9 %all_gather.19 = bf16[2048,16]{0,1:T(8,128)(2,1)S(1)} all-gather(bf16[256,16]{0,1:T(8,128)(2,1)S(1)} %copy-done.66), channel_id=1, replica_groups=mesh['expert'=4,'fsdp'=8] {'fsdp'}, dimensions={0}, use_global_device_ids=true | all-gather | bytes 73728 | tf_op jit(solution)/shard_map/all_gather | solution.py:70
  80.8 413.0 %all-gather.5.cloned.1.call-done = bf16[2048,6144]{1,0:T(8,128)(2,1)} async-done(((bf16[256,6144]{1,0:T(8,128)(2,1)}), bf16[2048,6144]{1,0:T(8,128)(2,1)}) %all-gather.5.cloned.1.call-update) | async-done | bytes 25165840 | tf_op jit(solution)/shard_map/all_gather | solution.py:68
  493.8 11.7 fusion.38
  505.5 1.9 slice_bitcast_fusion
  507.4 1.4 copy-done.20
  508.8 1.7 copy.226
  510.5 1.9 copy.188
  512.5 3.6 multiply_reduce_fusion.9
  517.1 3.3 copy.225
  520.4 3.4 copy.186
  523.8 2.9 multiply_reduce_fusion.10
  527.8 2.2 multiply_multiply_fusion
  535.6 2.1 convolution_convert_fusion.9
  537.7 83.1 %all-gather.7.cloned.1.call-done = bf16[2048,2048]{1,0:T(8,128)(2,1)} async-done(((bf16[256,2048]{1,0:T(8,128)(2,1)}), bf16[2048,2048]{1,0:T(8,128)(2,1)}) %all-gather.7.cloned.1.call-update) | async-done | bytes 8388624 | tf_op jit(solution)/shard_map/all_gather | solution.py:69
  620.8 5.8 multiply_reduce_fusion.8
  629.6 22.2 scatter_custom_fusion.1
  651.8 7.0 all-to-all-start.2
  659.4 21.2 scatter_custom_fusion
  680.6 161.2 %all-to-all-done.2 = bf16[16,256,2048]{2,1,0:T(8,128)(2,1)} async-done(((bf16[16,256,2048]{2,1,0:T(8,128)(2,1)}), bf16[16,256,2048]{2,1,0:T(8,128)(2,1)}, u32[]{:S(2)}, u32[]{:S(2)}) %all-to-all-start.2) | async-done | bytes 16777248 | tf_op jit(solution)/shard_map/all_to_all | solution.py:146
  841.9 7.6 all-to-all-start
  849.5 14.2 copy.199
  863.7 168.8 %all-to-all-done = bf16[16,256,2048]{2,1,0:T(8,128)(2,1)} async-done(((bf16[16,256,2048]{2,1,0:T(8,128)(2,1)}), bf16[16,256,2048]{2,1,0:T(8,128)(2,1)}, u32[]{:S(2)}, u32[]{:S(2)}) %all-to-all-start) | async-done | bytes 16777248 | tf_op jit(solution)/shard_map/all_to_all | solution.py:109
  1032.5 14.2 copy.195
  1046.7 211.6 %all-gather.9.cloned.1.call-done = bf16[4,2048,2048]{2,1,0:T(8,128)(2,1)} async-done(((bf16[4,256,2048]{2,1,0:T(8,128)(2,1)}), bf16[4,2048,2048]{2,1,0:T(8,128)(2,1)}) %all-gather.9.cloned.1.call-update) | async-done | bytes 33554448 | tf_op jit(solution)/shard_map/all_gather | solution.py:117
  1258.3 43.2 %fusion.53 = f32[4,1024,2048]{2,1,0:T(8,128)} fusion(bf16[4,1024,2048]{2,1,0:T(8,128)(2,1)} %bitcast.118, bf16[4,2048,2048]{2,1,0:T(8,128)(2,1)} %all-gather.9.cloned.1.call-done), kind=kOutput, calls=%fused_computation.138 | convolution fusion | flops 34359738368 | bytes 83886080 | tf_op jit(solution)/shard_map/erd,edf->erf/dot_general | solution.py:120
  1301.5 186.5 %all-gather.11.cloned.1.call-done = bf16[4,1024,2048]{2,1,0:T(8,128)(2,1)} async-done(((bf16[4,128,2048]{2,1,0:T(8,128)(2,1)}), bf16[4,1024,2048]{2,1,0:T(8,128)(2,1)}) %all-gather.11.cloned.1.call-update) | async-done | bytes 16777232 | tf_op jit(solution)/shard_map/all_gather | solution.py:118
  1488.0 37.0 %multiply_convert_fusion.1 = (bf16[4,1024,1024]{2,1,0:T(8,128)(2,1)}, bf16[4,1024,1024]{2,1,0:T(8,128)(2,1)}, bf16[4,1024,1024]{2,1,0:T(8,128)(2,1)}) fusion(f32[4,1024,2048]{2,1,0:T(8,128)} %fusion.53, bf16[4,1024,2048]{2,1,0:T(8,128)(2,1)} %bitcast.120, bf16[4,1024,2048]{2,1,0:T(8,128)(2,1)} %all-gather.11.cloned.1.call-done), kind=kOutput, calls=%fused_computation.15 | convolution fusion | flops 17246978048 | bytes 92274688 | tf_op jit(solution)/shard_map/erd,efd->erf/dot_general | solution.py:157
  1525.0 27.2 convolution_convert_fusion.4
  1552.2 22.1 copy.196
  1574.3 7.1 all-to-all-start.1
  1581.4 43.4 %convolution_convert_fusion.2 = bf16[4,1024,2048]{2,1,0:T(8,128)(2,1)} fusion(bf16[4,2048,2048]{2,1,0:T(8,128)(2,1)} %all-gather.9.cloned.1.call-done, bf16[4,1024,1024]{2,1,0:T(8,128)(2,1)} %get-tuple-element.30, bf16[4,1024,1024]{2,1,0:T(8,128)(2,1)} %get-tuple-element.29), kind=kOutput, calls=%fused_computation.18 | convolution fusion | flops 34401681408 | bytes 67108864 | tf_op jit(solution)/shard_map/erf,edf->erd/dot_general | solution.py:169
  1624.8 22.1 copy.202
  1646.9 117.5 %all-to-all-done.1 = bf16[4,1024,2048]{2,0,1:T(4,128)(2,1)} async-done(((bf16[4,1024,2048]{2,0,1:T(4,128)(2,1)}), bf16[4,1024,2048]{2,0,1:T(4,128)(2,1)}, u32[]{:S(2)}, u32[]{:S(2)}) %all-to-all-start.1) | async-done | bytes 16777248 | tf_op jit(solution)/shard_map/all_to_all | solution.py:130
  1764.5 7.2 all-to-all-start.3
  1771.8 18.6 copy.197
  1790.4 24.4 gather_fusion
  1814.8 9.5 fusion.1
  1824.5 130.2 %all-to-all-done.3 = bf16[4,1024,2048]{2,0,1:T(4,128)(2,1)} async-done(((bf16[4,1024,2048]{2,0,1:T(4,128)(2,1)}), bf16[4,1024,2048]{2,0,1:T(4,128)(2,1)}, u32[]{:S(2)}, u32[]{:S(2)}) %all-to-all-start.3) | async-done | bytes 16777248 | tf_op jit(solution)/shard_map/all_to_all | solution.py:172
  1954.7 18.6 copy.203
  1973.3 24.6 gather_fusion.1
  1998.0 11.4 convert_reduce_fusion
  2009.5 3.1 multiply_reduce_fusion.2
  2012.6 1.8 multiply_add_fusion
  2015.7 5.6 convolution_convert_fusion.5
  2022.9 6.1 convolution_convert_fusion.6
  2029.5 4.1 multiply_reduce_fusion
  2039.1 3.0 multiply_reduce_fusion.4
  2045.1 14.6 convolution_convert_fusion.1
  2061.9 27.1 convolution_convert_fusion.3
  2089.1 78.6 %reduce-scatter.8.cloned.1.call-done = bf16[256,2048]{1,0:T(8,128)(2,1)} async-done(((bf16[2048,2048]{1,0:T(8,128)(2,1)}), bf16[256,2048]{1,0:T(8,128)(2,1)}) %reduce-scatter.8.cloned.1.call-update) | async-done | bytes 1048592 | tf_op jit(solution)/shard_map/reduce_scatter | solution.py:245
  2167.7 407.0 %reduce-scatter.6.cloned.1.call-done = bf16[256,6144]{1,0:T(8,128)(2,1)} async-done(((bf16[2048,6144]{1,0:T(8,128)(2,1)}), bf16[256,6144]{1,0:T(8,128)(2,1)}) %reduce-scatter.6.cloned.1.call-update) | async-done | bytes 3145744 | tf_op jit(solution)/shard_map/reduce_scatter | solution.py:242
  2574.8 43.8 %convolution_convert_fusion = bf16[4,2048,2048]{2,1,0:T(8,128)(2,1)} fusion(bf16[4,1024,2048]{2,1,0:T(8,128)(2,1)} %bitcast.119, bf16[4,1024,1024]{2,1,0:T(8,128)(2,1)} %get-tuple-element.30, bf16[4,1024,1024]{2,1,0:T(8,128)(2,1)} %get-tuple-element.29), kind=kOutput, calls=%fused_computation.4 | convolution fusion | flops 34410070016 | bytes 67108864 | tf_op jit(solution)/shard_map/erd,erf->edf/dot_general | solution.py:166
  2618.7 14.2 fusion.22
  2633.0 43.8 %all-reduce = (f32[2048]{0:T(1024)}, f32[128]{0:T(128)}, f32[128]{0:T(128)}, f32[2048]{0:T(1024)}) all-reduce(f32[2048]{0:T(1024)S(1)} %get-tuple-element.19, f32[128]{0:T(128)S(1)} %copy-done.71, f32[128]{0:T(128)S(1)} %copy-done.72, f32[2048]{0:T(1024)S(1)} %copy-done.56), channel_id=1, replica_groups=mesh['expert'=4,'fsdp'=8] {'expert','fsdp'}, use_global_device_ids=true, to_apply=%region_22.0 | all-reduce | flops 4352 | bytes 34816 | tf_op jit(solution)/shard_map/psum | solution.py:257
  2676.8 3.5 fusion.21
  2680.2 6.7 psum.55
  2687.6 230.5 %reduce-scatter.14.cloned.1.call-done = bf16[4,128,2048]{2,1,0:T(8,128)(2,1)} async-done(((bf16[4,1024,2048]{2,1,0:T(8,128)(2,1)}), bf16[4,128,2048]{2,1,0:T(8,128)(2,1)}) %reduce-scatter.14.cloned.1.call-update) | async-done | bytes 2097168 | tf_op jit(solution)/shard_map/reduce_scatter | solution.py:179
  2918.1 4.1 convert_element_type.150
  2922.2 83.0 %all-reduce.4.cloned.1.call-done = (bf16[256,6144]{1,0:T(8,128)(2,1)}, bf16[256,2048]{1,0:T(8,128)(2,1)}) async-done(((bf16[256,6144]{1,0:T(8,128)(2,1)}, bf16[256,2048]{1,0:T(8,128)(2,1)}), (bf16[256,6144]{1,0:T(8,128)(2,1)}, bf16[256,2048]{1,0:T(8,128)(2,1)})) %all-reduce.4.cloned.1.call-update) | async-done | bytes 4194320 | tf_op jit(solution)/shard_map/psum | solution.py:253
  3005.3 2.9 convert_element_type.144
  3008.2 3.4 convert_element_type.142
  3011.6 541.0 %reduce-scatter.12.cloned.1.call-done = bf16[4,256,2048]{2,1,0:T(8,128)(2,1)} async-done(((bf16[4,2048,2048]{2,1,0:T(8,128)(2,1)}), bf16[4,256,2048]{2,1,0:T(8,128)(2,1)}) %reduce-scatter.12.cloned.1.call-update) | async-done | bytes 4194320 | tf_op jit(solution)/shard_map/reduce_scatter | solution.py:176
  3552.6 6.7 convert_element_type.148
  (215 shorter events, 29.8 us)
Async XLA Ops:
  7.2 486.6 %all-gather.5.cloned.1.call-start = ((), (), s32[]{:S(2)}) async-start(), calls=%async_computation.9 | async-start | bytes 28311552 | tf_op jit(solution)/shard_map/all_gather | solution.py:68
  7.2 2.2 copy-start.54
  7.2 2.2 copy-start.65
  7.2 2.5 copy-start.26
  7.9 3.4 copy-start.66
  7.9 612.9 %all-gather.7.cloned.1.call-start = ((), (), s32[]{:S(2)}) async-start(), calls=%async_computation.10 | async-start | bytes 9437184 | tf_op jit(solution)/shard_map/all_gather | solution.py:69
  8.7 71.8 %copy-start.14 = (bf16[256,2048]{1,0:T(8,128)(2,1)S(1)}, bf16[256,2048]{1,0:T(8,128)(2,1)}, u32[]{:S(2)}) copy-start(bf16[256,2048]{1,0:T(8,128)(2,1)} %param.13) | copy-start | bytes 3145732
  8.7 485.1 %copy-start.34 = (f32[2048]{0:T(1024)S(1)}, f32[2048]{0:T(1024)}, u32[]{:S(2)}) copy-start(f32[2048]{0:T(1024)} %param.16) | copy-start | bytes 24580
  8.7 1249.6 %all-gather.9.cloned.1.call-start = ((), (), s32[]{:S(2)}) async-start(), calls=%async_computation.11 | async-start | bytes 37748736 | tf_op jit(solution)/shard_map/all_gather | solution.py:117
  79.2 549.1 %copy-start.36 = (bf16[2048,16]{0,1:T(8,128)(2,1)}, bf16[2048,16]{0,1:T(8,128)(2,1)S(1)}, u32[]{:S(2)}) copy-start(bf16[2048,16]{0,1:T(8,128)(2,1)S(1)} %all_gather.19) | copy-start | bytes 196612
  80.8 424.7 %copy-start.50 = (f32[256]{0:T(256)}, f32[256]{0:T(256)S(1)}, u32[]{:S(2)}) copy-start(f32[256]{0:T(256)S(1)} %add_rsqrt_fusion.3) | copy-start | bytes 3076
  80.8 578.6 %copy-start.57 = (s32[2048,1]{0,1:T(1,128)}, s32[2048,1]{0,1:T(1,128)S(1)}, u32[]{:S(2)}) copy-start(s32[2048,1]{0,1:T(1,128)S(1)} %compare_select_fusion) | copy-start | bytes 24580
  505.5 3.3 copy-start.20
  512.5 15.3 copy-start.4
  520.4 7.3 copy-start.67
  520.4 7.4 copy-start.69
  527.7 2.3 copy-start.44
  527.7 2.2 copy-start.46
  537.7 83.1 %copy-start.18 = (bf16[16,128,256]{2,1,0:T(8,128)(2,1)}, bf16[16,128,256]{2,1,0:T(8,128)(2,1)S(1)}, u32[]{:S(2)}) copy-start(bf16[16,128,256]{2,1,0:T(8,128)(2,1)S(1)} %convolution_convert_fusion.9) | copy-start | bytes 3145732
  620.8 7.2 copy-start.52
  626.7 2.9 copy-start.10
  626.7 25.1 copy-start.61
  628.3 31.2 copy-start.16
  629.3 22.5 copy-start.63
  629.5 22.3 copy-start.32
  651.8 190.1 %all-to-all-start.2 = ((bf16[16,256,2048]{2,1,0:T(8,128)(2,1)}), bf16[16,256,2048]{2,1,0:T(8,128)(2,1)}, u32[]{:S(2)}, u32[]{:S(2)}) async-start(bf16[16,256,2048]{2,1,0:T(8,128)(2,1)} %bitcast.113), calls=%async_computation.2 | async-start | bytes 33554432 | tf_op jit(solution)/shard_map/all_to_all | solution.py:146
  658.8 829.2 %all-gather.11.cloned.1.call-start = ((), (), s32[]{:S(2)}) async-start(), calls=%async_computation.12 | async-start | bytes 18874368 | tf_op jit(solution)/shard_map/all_gather | solution.py:118
  841.9 190.6 %all-to-all-start = ((bf16[16,256,2048]{2,1,0:T(8,128)(2,1)}), bf16[16,256,2048]{2,1,0:T(8,128)(2,1)}, u32[]{:S(2)}, u32[]{:S(2)}) async-start(bf16[16,256,2048]{2,1,0:T(8,128)(2,1)} %bitcast.112), calls=%async_computation | async-start | bytes 33554432 | tf_op jit(solution)/shard_map/all_to_all | solution.py:109
  1574.3 190.1 %all-to-all-start.1 = ((bf16[4,1024,2048]{2,0,1:T(4,128)(2,1)}), bf16[4,1024,2048]{2,0,1:T(4,128)(2,1)}, u32[]{:S(2)}, u32[]{:S(2)}) async-start(bf16[4,1024,2048]{2,0,1:T(4,128)(2,1)} %copy.196), calls=%async_computation.1 | async-start | bytes 33554432 | tf_op jit(solution)/shard_map/all_to_all | solution.py:130
  1646.9 124.8 %copy-start.58 = (s32[2048,1]{0,1:T(1,128)S(1)}, s32[2048,1]{0,1:T(1,128)}, u32[]{:S(2)}) copy-start(s32[2048,1]{0,1:T(1,128)} %copy-done.57) | copy-start | bytes 24580
  1764.5 190.3 %all-to-all-start.3 = ((bf16[4,1024,2048]{2,0,1:T(4,128)(2,1)}), bf16[4,1024,2048]{2,0,1:T(4,128)(2,1)}, u32[]{:S(2)}, u32[]{:S(2)}) async-start(bf16[4,1024,2048]{2,0,1:T(4,128)(2,1)} %copy.202), calls=%async_computation.3 | async-start | bytes 33554432 | tf_op jit(solution)/shard_map/all_to_all | solution.py:172
  1771.7 396.0 %reduce-scatter.8.cloned.1.call-start = ((), (), s32[]{:S(2)}) async-start(), calls=%async_computation.14 | async-start | bytes 9437184 | tf_op jit(solution)/shard_map/reduce_scatter | solution.py:245
  1790.4 24.4 copy-start.11
  1790.4 24.4 copy-start.33
  1814.8 9.6 copy-start.41
  1814.8 9.6 copy-start.60
  1814.8 9.6 copy-start.64
  1814.8 9.6 copy-start.55
  1998.0 11.4 copy-start.3
  1998.0 11.4 copy-start.37
  1998.0 11.4 copy-start.53
  1998.0 11.4 copy-start.62
  2009.4 3.1 copy-start.25
  2009.4 3.1 copy-start.27
  2012.6 3.1 copy-start.19
  2021.3 553.5 %reduce-scatter.6.cloned.1.call-start = ((), (), s32[]{:S(2)}) async-start(), calls=%async_computation.13 | async-start | bytes 28311552 | tf_op jit(solution)/shard_map/reduce_scatter | solution.py:242
  2029.5 4.1 copy-start.1
  2036.9 2.2 copy-start.6
  2036.9 2.2 copy-start.38
  2036.9 2.2 copy-start.45
  2036.9 2.2 copy-start.47
  2036.9 2.2 copy-start.68
  2036.9 2.2 copy-start.70
  2039.1 3.0 copy-start.13
  2042.9 2.1 copy-start.15
  2059.8 620.5 %reduce-scatter.10.cloned.1.call-start = ((), (), s32[]{:S(2)}) async-start(), calls=%async_computation.15 | async-start | bytes 73728 | tf_op jit(solution)/shard_map/reduce_scatter | solution.py:248
  2061.8 856.2 %reduce-scatter.14.cloned.1.call-start = ((), (), s32[]{:S(2)}) async-start(), calls=%async_computation.17 | async-start | bytes 18874368 | tf_op jit(solution)/shard_map/reduce_scatter | solution.py:179
  2089.1 916.2 %all-reduce.4.cloned.1.call-start = ((), (), s32[]{:S(2)}) async-start(), calls=%async_computation.18 | async-start | bytes 8388608 | tf_op jit(solution)/shard_map/psum | solution.py:253
  2574.8 977.9 %reduce-scatter.12.cloned.1.call-start = ((), (), s32[]{:S(2)}) async-start(), calls=%async_computation.16 | async-start | bytes 37748736 | tf_op jit(solution)/shard_map/reduce_scatter | solution.py:176
  2618.7 14.3 copy-start.56
  2618.7 14.3 copy-start.71
  2618.7 14.3 copy-start.72
  2618.7 58.1 %copy-start.9 = (f32[256,2048]{1,0:T(8,128)S(1)}, f32[256,2048]{1,0:T(8,128)}, u32[]{:S(2)}) copy-start(f32[256,2048]{1,0:T(8,128)} %copy-done.7) | copy-start | bytes 6291460
  3005.3 2.9 copy-start.31
  (23 other events, 30.5 us)
Sparse Core Ops, SparseCore 0:
  9.5 484.1 all-gather.4
  495.9 124.8 all-gather.6
  622.4 635.9 all-gather.8
  1260.4 227.5 all-gather.10
  2021.4 146.2 reduce-scatter.7
  2171.9 402.7 reduce-scatter.5
  2578.2 52.8 reduce-scatter.9
  2635.3 282.7 reduce-scatter.13
  2920.5 84.6 all-reduce.3
  3009.3 543.2 reduce-scatter.11
where the time goes:
time: 3570 us
  waiting for transfers between devices  2810 us (79%)
  matrix products  293 us (8%)
  local copies, waits for them, and re-layouts  208 us (6%)
  blocking collectives  118 us (3%)
  other arithmetic  87 us (2%)
    reduce_scatter x1, waiting for transfers between devices, local(): lax.psum_scatter(gate_up_grad_full.astype(jnp.bfloat16), 'fsdp', scatter_...  541 us
    all_gather x1, waiting for transfers between devices, local(): lax.all_gather(qkv_weight, 'fsdp', axis=0, tiled=True)  413 us
    reduce_scatter x1, waiting for transfers between devices, local(): lax.psum_scatter(qkv_grad_full.astype(jnp.bfloat16), 'fsdp', scatter_dime...  407 us
    reduce_scatter x1, waiting for transfers between devices, local(): lax.psum_scatter(down_grad_full.astype(jnp.bfloat16), 'fsdp', scatter_dim...  231 us
    all_gather x1, waiting for transfers between devices, local(): lax.all_gather(gate_up_weight, 'fsdp', axis=1, tiled=True)  212 us
    all_gather x1, waiting for transfers between devices, local(): lax.all_gather(down_weight, 'fsdp', axis=1, tiled=True)  187 us
    all_to_all x1, waiting for transfers between devices, local(): lax.all_to_all(outgoing.reshape(experts, capacity, model_width), 'expert'...  169 us
    all_to_all x1, waiting for transfers between devices, local(): lax.all_to_all(grad_out.reshape(experts, capacity, model_width), 'expert'...  161 us
  transfers between devices with their start and end apart: 14, of which 13 were waited for; matrix products, arithmetic and copies ran while one was open for 12% of the time, Pallas kernels for 0%

commit v1 on v0

--- a/solution.py
+++ b/solution.py
@@ -5,6 +5,19 @@
 
 EPSILON = 1e-06
 ROPE_BASE = 50000.0
+
+
+def gather_around(shard, axis, dim):
+    ways = lax.axis_size(axis)
+    up = [(d, (d + 1) % ways) for d in range(ways)]
+    down = [(d, (d - 1) % ways) for d in range(ways)]
+    earlier, later = ([shard], [shard])
+    for _ in range(ways // 2):
+        earlier.append(lax.ppermute(earlier[-1], axis, up))
+    for _ in range((ways - 1) // 2):
+        later.append(lax.ppermute(later[-1], axis, down))
+    line = jnp.concatenate([*earlier[::-1], *later[1:]], axis=dim)
+    return jnp.roll(line, (lax.axis_index(axis) - ways // 2) * shard.shape[dim], axis=dim)
 
 
 def normalize(values):
@@ -114,7 +127,7 @@
         tiled=True,
     )
     gate_up_full, down_full = (
-        lax.all_gather(gate_up_weight, "fsdp", axis=1, tiled=True),
+        gather_around(gate_up_weight, "fsdp", 1),
         lax.all_gather(down_weight, "fsdp", axis=1, tiled=True),
     )
     gate_up_val = jnp.einsum(

time: 3570 us -> 4260 us (1.19)
  blocking collectives: 118 us -> 432 us
  waiting for transfers between devices: 2810 us -> 3100 us
  local copies, waits for them, and re-layouts: 208 us -> 275 us
    ppermute x0 -> x7, waiting for transfers between devices: none -> 852 us  [the longest x3 490 us: gather_around(): later.append(lax.ppermute(later[-1], axis, down))]
    all_gather x1, blocking collectives: 67.9 us -> 383 us  [local(): lax.all_gather(router_weight, 'fsdp', axis=0, tiled=True)]
    all_gather x1, waiting for transfers between devices: 212 us -> 0.02 us  [local(): lax.all_gather(gate_up_weight, 'fsdp', axis=1, tiled=True)]
    all_gather x1, waiting for transfers between devices: 187 us -> 0.01 us  [local(): lax.all_gather(down_weight, 'fsdp', axis=1, tiled=True)]
    all_to_all x1, waiting for transfers between devices: 169 us -> 0.01 us  [local(): lax.all_to_all(outgoing.reshape(experts, capacity, model_width), 'expert'...]
    all_to_all x1, waiting for transfers between devices: 161 us -> 0.01 us  [local(): lax.all_to_all(grad_out.reshape(experts, capacity, model_width), 'expert'...]
    reduce_scatter x1, waiting for transfers between devices: 78.6 us -> 167 us  [local(): lax.psum_scatter(out_grad_full.astype(jnp.bfloat16), 'fsdp', scatter_dime...]
    all_gather x1, waiting for transfers between devices: 413 us -> 481 us  [local(): lax.all_gather(qkv_weight, 'fsdp', axis=0, tiled=True)]
  transfers between devices with their start and end apart: 14 -> 21, of which waited for: 13 -> 15; matrix products, arithmetic and copies ran while one was open for 12% -> 13% of each run, Pallas kernels for 0% -> 0%
where the time goes in v1:
time: 4260 us; the launch traced here: 4250 us
  waiting for transfers between devices  3100 us (73%)
  blocking collectives  432 us (10%)
  matrix products  294 us (7%)
  local copies, waits for them, and re-layouts  275 us (6%)
  other arithmetic  88 us (2%)
  starting transfers between devices  49.7 us (1%)
    reduce_scatter x1, waiting for transfers between devices, local(): lax.psum_scatter(gate_up_grad_full.astype(jnp.bfloat16), 'fsdp', scatter_...  540 us
    ppermute x3, waiting for transfers between devices, gather_around(): later.append(lax.ppermute(later[-1], axis, down))  490 us
    all_gather x1, waiting for transfers between devices, local(): lax.all_gather(qkv_weight, 'fsdp', axis=0, tiled=True)  481 us
    reduce_scatter x1, waiting for transfers between devices, local(): lax.psum_scatter(qkv_grad_full.astype(jnp.bfloat16), 'fsdp', scatter_dime...  407 us
    all_gather x1, blocking collectives, local(): lax.all_gather(router_weight, 'fsdp', axis=0, tiled=True)  383 us
    ppermute x4, waiting for transfers between devices, gather_around(): earlier.append(lax.ppermute(earlier[-1], axis, up))  362 us
    reduce_scatter x1, waiting for transfers between devices, local(): lax.psum_scatter(down_grad_full.astype(jnp.bfloat16), 'fsdp', scatter_dim...  218 us
    reduce_scatter x1, waiting for transfers between devices, local(): lax.psum_scatter(out_grad_full.astype(jnp.bfloat16), 'fsdp', scatter_dime...  167 us
  transfers between devices with their start and end apart: 21, of which 15 were waited for; matrix products, arithmetic and copies ran while one was open for 13% of the time, Pallas kernels for 0%

profile of v1, /device:TPU:0, one launch (start us, length us, event | category | flops | bytes accessed | tf_op | source)
XLA Modules:
  0.0 4251.0 jit_solution(7285428233649535093)
XLA Ops:
  11.9 480.8 %all-gather.5.cloned.1.call-done = bf16[2048,6144]{1,0:T(8,128)(2,1)} async-done(((bf16[256,6144]{1,0:T(8,128)(2,1)}), bf16[2048,6144]{1,0:T(8,128)(2,1)}) %all-gather.5.cloned.1.call-update) | async-done | bytes 25165840 | tf_op jit(solution)/shard_map/all_gather | solution.py:81
  492.7 11.7 fusion.40
  533.9 85.8 %all-gather.7.cloned.1.call-done = bf16[2048,2048]{1,0:T(8,128)(2,1)} async-done(((bf16[256,2048]{1,0:T(8,128)(2,1)}), bf16[2048,2048]{1,0:T(8,128)(2,1)}) %all-gather.7.cloned.1.call-update) | async-done | bytes 8388624 | tf_op jit(solution)/shard_map/all_gather | solution.py:82
  619.8 5.8 multiply_reduce_fusion.8
  627.2 21.4 scatter_custom_fusion
  648.6 7.2 all-to-all-start
  656.4 177.6 %collective-permute-done = bf16[4,256,2048]{2,1,0:T(8,128)(2,1)S(1)} collective-permute-done((bf16[4,256,2048]{2,1,0:T(8,128)(2,1)}, bf16[4,256,2048]{2,1,0:T(8,128)(2,1)S(1)}, u32[]{:S(2)}, u32[]{:S(2)}) %collective-permute-start) | collective-permute-done | bytes 4194336 | tf_op jit(solution)/shard_map/ppermute | solution.py:16
  834.0 4.7 collective-permute-start.4
  838.7 179.5 %collective-permute-done.1 = bf16[4,256,2048]{2,1,0:T(8,128)(2,1)} collective-permute-done((bf16[4,256,2048]{2,1,0:T(8,128)(2,1)S(1)}, bf16[4,256,2048]{2,1,0:T(8,128)(2,1)}, u32[]{:S(2)}, u32[]{:S(2)}) %collective-permute-start.1) | collective-permute-done | bytes 4194336 | tf_op jit(solution)/shard_map/ppermute | solution.py:16
  1021.5 382.8 %all_gather.18 = bf16[2048,16]{0,1:T(8,128)(2,1)S(1)} all-gather(bf16[256,16]{0,1:T(8,128)(2,1)S(1)} %copy-done.69), channel_id=1, replica_groups=mesh['expert'=4,'fsdp'=8] {'fsdp'}, dimensions={0}, use_global_device_ids=true | all-gather | bytes 73728 | tf_op jit(solution)/shard_map/all_gather | solution.py:83
  1406.4 22.5 scatter_custom_fusion.1
  1428.9 7.0 all-to-all-start.2
  1438.0 351.1 %collective-permute-done.5 = bf16[4,256,2048]{2,1,0:T(8,128)(2,1)} collective-permute-done((bf16[4,256,2048]{2,1,0:T(8,128)(2,1)}, bf16[4,256,2048]{2,1,0:T(8,128)(2,1)}, u32[]{:S(2)}, u32[]{:S(2)}) %collective-permute-start.5) | collective-permute-done | bytes 4194336 | tf_op jit(solution)/shard_map/ppermute | solution.py:18
  1789.1 11.1 collective-permute-start.6
  1800.2 4.6 collective-permute-done.3
  1804.8 4.9 constant_dynamic-update-slice_fusion.15
  1809.7 4.9 constant_dynamic-update-slice_fusion.14
  1814.6 5.0 constant_dynamic-update-slice_fusion.13
  1825.7 4.9 constant_dynamic-update-slice_fusion.10
  1830.6 4.9 constant_dynamic-update-slice_fusion.9
  1835.5 138.8 %collective-permute-done.6 = bf16[4,256,2048]{2,1,0:T(8,128)(2,1)} collective-permute-done((bf16[4,256,2048]{2,1,0:T(8,128)(2,1)}, bf16[4,256,2048]{2,1,0:T(8,128)(2,1)}, u32[]{:S(2)}, u32[]{:S(2)}) %collective-permute-start.6) | collective-permute-done | bytes 4194336 | tf_op jit(solution)/shard_map/ppermute | solution.py:18
  1974.3 5.0 constant_dynamic-update-slice_fusion.8
  1979.3 5.0 constant_dynamic-update-slice_fusion.7
  1984.3 4.8 constant_dynamic-update-slice_fusion.6
  1989.2 4.8 constant_dynamic-update-slice_fusion.5
  1998.8 4.8 constant_dynamic-update-slice_fusion.2
  2003.6 4.8 constant_dynamic-update-slice_fusion.1
  2008.4 4.8 constant_dynamic-update-slice_fusion
  2013.3 14.3 copy.195
  2027.6 14.1 copy.199
  2041.7 43.2 %fusion = f32[4,1024,2048]{2,1,0:T(8,128)} fusion(bf16[4,1024,2048]{2,1,0:T(8,128)(2,1)} %bitcast.115, bf16[4,4096,2048]{2,1,0:T(8,128)(2,1)} %constant_dynamic-update-slice_fusion, s32[]{:T(128)S(6)} %select_n.28), kind=kOutput, calls=%fused_computation.4 | convolution fusion | flops 34359738368 | bytes 83886080 | tf_op jit(solution)/shard_map/erd,edf->erf/dot_general | solution.py:133
  2084.9 37.0 multiply_convert_fusion.1
  2121.9 27.3 convolution_convert_fusion.4
  2149.2 22.1 copy.196
  2171.3 7.0 all-to-all-start.1
  2178.3 43.3 %convolution_convert_fusion.2 = bf16[4,1024,2048]{2,1,0:T(8,128)(2,1)} fusion(bf16[4,2048,2048]{2,1,0:T(8,128)(2,1)} %all-gather.11.cloned.1.call-done, bf16[4,1024,1024]{2,1,0:T(8,128)(2,1)} %get-tuple-element.30, bf16[4,1024,1024]{2,1,0:T(8,128)(2,1)} %get-tuple-element.29), kind=kOutput, calls=%fused_computation.20 | convolution fusion | flops 34401681408 | bytes 67108864 | tf_op jit(solution)/shard_map/erf,edf->erd/dot_general | solution.py:182
  2221.6 22.2 copy.202
  2243.8 117.5 %all-to-all-done.1 = bf16[4,1024,2048]{2,0,1:T(4,128)(2,1)} async-done(((bf16[4,1024,2048]{2,0,1:T(4,128)(2,1)}), bf16[4,1024,2048]{2,0,1:T(4,128)(2,1)}, u32[]{:S(2)}, u32[]{:S(2)}) %all-to-all-start.1) | async-done | bytes 16777248 | tf_op jit(solution)/shard_map/all_to_all | solution.py:143
  2361.3 7.4 all-to-all-start.3
  2368.8 18.6 copy.197
  2387.5 24.4 gather_fusion
  2411.9 9.5 fusion.3
  2421.6 130.3 %all-to-all-done.3 = bf16[4,1024,2048]{2,0,1:T(4,128)(2,1)} async-done(((bf16[4,1024,2048]{2,0,1:T(4,128)(2,1)}), bf16[4,1024,2048]{2,0,1:T(4,128)(2,1)}, u32[]{:S(2)}, u32[]{:S(2)}) %all-to-all-start.3) | async-done | bytes 16777248 | tf_op jit(solution)/shard_map/all_to_all | solution.py:185
  2551.8 18.6 copy.203
  2570.4 24.4 gather_fusion.1
  2594.9 11.4 convert_reduce_fusion
  2612.6 5.6 convolution_convert_fusion.5
  2619.8 5.7 convolution_convert_fusion.6
  2626.1 4.0 multiply_reduce_fusion
  2641.6 14.6 convolution_convert_fusion.1
  2658.4 26.8 convolution_convert_fusion.3
  2685.3 166.7 %reduce-scatter.8.cloned.1.call-done = bf16[256,2048]{1,0:T(8,128)(2,1)} async-done(((bf16[2048,2048]{1,0:T(8,128)(2,1)}), bf16[256,2048]{1,0:T(8,128)(2,1)}) %reduce-scatter.8.cloned.1.call-update) | async-done | bytes 1048592 | tf_op jit(solution)/shard_map/reduce_scatter | solution.py:258
  2852.0 406.9 %reduce-scatter.6.cloned.1.call-done = bf16[256,6144]{1,0:T(8,128)(2,1)} async-done(((bf16[2048,6144]{1,0:T(8,128)(2,1)}), bf16[256,6144]{1,0:T(8,128)(2,1)}) %reduce-scatter.6.cloned.1.call-update) | async-done | bytes 3145744 | tf_op jit(solution)/shard_map/reduce_scatter | solution.py:255
  3259.0 43.9 %convolution_convert_fusion = bf16[4,2048,2048]{2,1,0:T(8,128)(2,1)} fusion(bf16[4,1024,2048]{2,1,0:T(8,128)(2,1)} %bitcast.116, bf16[4,1024,1024]{2,1,0:T(8,128)(2,1)} %get-tuple-element.30, bf16[4,1024,1024]{2,1,0:T(8,128)(2,1)} %get-tuple-element.29), kind=kOutput, calls=%fused_computation.6 | convolution fusion | flops 34410070016 | bytes 67108864 | tf_op jit(solution)/shard_map/erd,erf->edf/dot_general | solution.py:179
  3302.9 13.0 reduce-scatter.10.cloned.1.call-done
  3315.9 5.9 psum.55
  3322.4 14.9 fusion.24
  3337.3 43.8 %all-reduce = (f32[2048]{0:T(1024)}, f32[128]{0:T(128)}, f32[128]{0:T(128)}, f32[2048]{0:T(1024)}) all-reduce(f32[2048]{0:T(1024)S(1)} %get-tuple-element.19, f32[128]{0:T(128)S(1)} %copy-done.72, f32[128]{0:T(128)S(1)} %copy-done.73, f32[2048]{0:T(1024)S(1)} %copy-done.59), channel_id=1, replica_groups=mesh['expert'=4,'fsdp'=8] {'expert','fsdp'}, use_global_device_ids=true, to_apply=%region_22.23 | all-reduce | flops 4352 | bytes 34816 | tf_op jit(solution)/shard_map/psum | solution.py:270
  3384.6 218.3 %reduce-scatter.14.cloned.1.call-done = bf16[4,128,2048]{2,1,0:T(8,128)(2,1)} async-done(((bf16[4,1024,2048]{2,1,0:T(8,128)(2,1)}), bf16[4,128,2048]{2,1,0:T(8,128)(2,1)}) %reduce-scatter.14.cloned.1.call-update) | async-done | bytes 2097168 | tf_op jit(solution)/shard_map/reduce_scatter | solution.py:192
  3602.8 4.1 convert_element_type.150
  3607.0 83.0 %all-reduce.4.cloned.1.call-done = (bf16[256,6144]{1,0:T(8,128)(2,1)}, bf16[256,2048]{1,0:T(8,128)(2,1)}) async-done(((bf16[256,6144]{1,0:T(8,128)(2,1)}, bf16[256,2048]{1,0:T(8,128)(2,1)}), (bf16[256,6144]{1,0:T(8,128)(2,1)}, bf16[256,2048]{1,0:T(8,128)(2,1)})) %all-reduce.4.cloned.1.call-update) | async-done | bytes 4194320 | tf_op jit(solution)/shard_map/psum | solution.py:266
  3690.0 5.4 convert_element_type.142
  3697.0 540.3 %reduce-scatter.12.cloned.1.call-done = bf16[4,256,2048]{2,1,0:T(8,128)(2,1)} async-done(((bf16[4,2048,2048]{2,1,0:T(8,128)(2,1)}), bf16[4,256,2048]{2,1,0:T(8,128)(2,1)}) %reduce-scatter.12.cloned.1.call-update) | async-done | bytes 4194320 | tf_op jit(solution)/shard_map/reduce_scatter | solution.py:189
  4237.3 6.7 convert_element_type.148
  (247 shorter events, 82.1 us)
Async XLA Ops:
  7.2 485.5 %all-gather.5.cloned.1.call-start = ((), (), s32[]{:S(2)}) async-start(), calls=%async_computation.9 | async-start | bytes 28311552 | tf_op jit(solution)/shard_map/all_gather | solution.py:81
  7.9 3.6 copy-start.16
  7.9 611.8 %all-gather.7.cloned.1.call-start = ((), (), s32[]{:S(2)}) async-start(), calls=%async_computation.10 | async-start | bytes 9437184 | tf_op jit(solution)/shard_map/all_gather | solution.py:82
  8.7 484.0 %copy-start.37 = (f32[2048]{0:T(1024)S(1)}, f32[2048]{0:T(1024)}, u32[]{:S(2)}) copy-start(f32[2048]{0:T(1024)} %param.16) | copy-start | bytes 24580
  8.7 2076.2 %all-gather.9.cloned.1.call-start = ((), (), s32[]{:S(2)}) async-start(), calls=%async_computation.11 | async-start | bytes 18874368 | tf_op jit(solution)/shard_map/all_gather | solution.py:131
  9.4 2168.9 %all-gather.11.cloned.1.call-start = ((), (), s32[]{:S(2)}) async-start(), calls=%async_computation.12 | async-start | bytes 37748736 | tf_op jit(solution)/shard_map/all_gather | solution.py:167
  11.9 492.6 %copy-start.53 = (f32[256]{0:T(256)}, f32[256]{0:T(256)S(1)}, u32[]{:S(2)}) copy-start(f32[256]{0:T(256)S(1)} %add_rsqrt_fusion.3) | copy-start | bytes 3076
  11.9 1394.5 %copy-start.60 = (s32[2048,1]{0,1:T(1,128)}, s32[2048,1]{0,1:T(1,128)S(1)}, u32[]{:S(2)}) copy-start(s32[2048,1]{0,1:T(1,128)S(1)} %compare_select_fusion) | copy-start | bytes 24580
  504.4 3.3 copy-start.24
  508.2 5.3 copy-start.15
  515.9 10.3 copy-start.5
  523.2 3.0 copy-start.47
  524.0 2.3 copy-start.49
  533.9 91.7 %copy-start.22 = (bf16[16,128,256]{2,1,0:T(8,128)(2,1)}, bf16[16,128,256]{2,1,0:T(8,128)(2,1)S(1)}, u32[]{:S(2)}) copy-start(bf16[16,128,256]{2,1,0:T(8,128)(2,1)S(1)} %convolution_convert_fusion.9) | copy-start | bytes 3145732
  619.8 7.2 copy-start.55
  625.6 22.9 copy-start.64
  627.2 777.1 %copy-start.18 = (bf16[256,2048]{1,0:T(8,128)(2,1)}, bf16[256,2048]{1,0:T(8,128)(2,1)S(1)}, u32[]{:S(2)}) copy-start(bf16[256,2048]{1,0:T(8,128)(2,1)S(1)} %multiply_convert_fusion.6) | copy-start | bytes 3145732
  648.6 372.9 %copy-start.69 = (bf16[256,16]{0,1:T(8,128)(2,1)S(1)}, bf16[256,16]{0,1:T(8,128)(2,1)}, u32[]{:S(2)}) copy-start(bf16[256,16]{0,1:T(8,128)(2,1)} %param.22) | copy-start | bytes 24580
  648.6 780.3 %all-to-all-start = ((bf16[16,256,2048]{2,1,0:T(8,128)(2,1)}), bf16[16,256,2048]{2,1,0:T(8,128)(2,1)}, u32[]{:S(2)}, u32[]{:S(2)}) async-start(bf16[16,256,2048]{2,1,0:T(8,128)(2,1)} %bitcast.109), calls=%async_computation | async-start | bytes 33554432 | tf_op jit(solution)/shard_map/all_to_all | solution.py:122
  655.7 178.2 %collective-permute-start = (bf16[4,256,2048]{2,1,0:T(8,128)(2,1)}, bf16[4,256,2048]{2,1,0:T(8,128)(2,1)S(1)}, u32[]{:S(2)}, u32[]{:S(2)}) collective-permute-start(bf16[4,256,2048]{2,1,0:T(8,128)(2,1)} %param.23), channel_id=1, source_target_pairs={{0,1},{1,2},{2,3},{3,4},{4,5},{5,6},{6,7},{7,0},{8,9},{9,10},{10,1... | collective-permute-start | bytes 12582920 | tf_op jit(solution)/shard_map/ppermute | solution.py:16
  834.0 184.2 %copy-start.20 = (bf16[4,256,2048]{2,1,0:T(8,128)(2,1)}, bf16[4,256,2048]{2,1,0:T(8,128)(2,1)S(1)}, u32[]{:S(2)}) copy-start(bf16[4,256,2048]{2,1,0:T(8,128)(2,1)S(1)} %collective-permute-done) | copy-start | bytes 12582916
  834.0 184.2 %collective-permute-start.1 = (bf16[4,256,2048]{2,1,0:T(8,128)(2,1)S(1)}, bf16[4,256,2048]{2,1,0:T(8,128)(2,1)}, u32[]{:S(2)}, u32[]{:S(2)}) collective-permute-start(bf16[4,256,2048]{2,1,0:T(8,128)(2,1)S(1)} %collective-permute-done), channel_id=1, source_target_pairs={{0,1},{1,2},{2,3},{3,4},{4,5},{5,6},{6,7},{7,0},{8,9},{9,10},{10,1... | collective-permute-start | bytes 12582920 | tf_op jit(solution)/shard_map/ppermute | solution.py:16
  834.0 601.9 %collective-permute-start.4 = (bf16[4,256,2048]{2,1,0:T(8,128)(2,1)}, bf16[4,256,2048]{2,1,0:T(8,128)(2,1)}, u32[]{:S(2)}, u32[]{:S(2)}) collective-permute-start(bf16[4,256,2048]{2,1,0:T(8,128)(2,1)} %param.23), channel_id=1, source_target_pairs={{0,7},{1,0},{2,1},{3,2},{4,3},{5,4},{6,5},{7,6},{8,15},{9,8},{10,9... | collective-permute-start | bytes 12582920 | tf_op jit(solution)/shard_map/ppermute | solution.py:18
  1018.2 417.8 %collective-permute-start.2 = (bf16[4,256,2048]{2,1,0:T(8,128)(2,1)}, bf16[4,256,2048]{2,1,0:T(8,128)(2,1)}, u32[]{:S(2)}, u32[]{:S(2)}) collective-permute-start(bf16[4,256,2048]{2,1,0:T(8,128)(2,1)} %collective-permute-done.1), channel_id=1, source_target_pairs={{0,1},{1,2},{2,3},{3,4},{4,5},{5,6},{6,7},{7,0},{8,9},{9,10},{10,1... | collective-permute-start | bytes 12582920 | tf_op jit(solution)/shard_map/ppermute | solution.py:16
  1021.5 407.3 %copy-start.11 = (f32[256,2048]{1,0:T(8,128)}, f32[256,2048]{1,0:T(8,128)S(1)}, u32[]{:S(2)}) copy-start(f32[256,2048]{1,0:T(8,128)S(1)} %convert_element_type.132) | copy-start | bytes 6291460
  1406.2 22.6 copy-start.34
  1428.9 598.7 %all-to-all-start.2 = ((bf16[16,256,2048]{2,1,0:T(8,128)(2,1)}), bf16[16,256,2048]{2,1,0:T(8,128)(2,1)}, u32[]{:S(2)}, u32[]{:S(2)}) async-start(bf16[16,256,2048]{2,1,0:T(8,128)(2,1)} %bitcast.110), calls=%async_computation.2 | async-start | bytes 33554432 | tf_op jit(solution)/shard_map/all_to_all | solution.py:159
  1435.9 353.2 %collective-permute-start.5 = (bf16[4,256,2048]{2,1,0:T(8,128)(2,1)}, bf16[4,256,2048]{2,1,0:T(8,128)(2,1)}, u32[]{:S(2)}, u32[]{:S(2)}) collective-permute-start(bf16[4,256,2048]{2,1,0:T(8,128)(2,1)} %collective-permute-done.4), channel_id=1, source_target_pairs={{0,7},{1,0},{2,1},{3,2},{4,3},{5,4},{6,5},{7,6},{8,15},{9,8},{10,9... | collective-permute-start | bytes 12582920 | tf_op jit(solution)/shard_map/ppermute | solution.py:18
  1436.0 368.8 %collective-permute-start.3 = (bf16[4,256,2048]{2,1,0:T(8,128)(2,1)}, bf16[4,256,2048]{2,1,0:T(8,128)(2,1)}, u32[]{:S(2)}, u32[]{:S(2)}) collective-permute-start(bf16[4,256,2048]{2,1,0:T(8,128)(2,1)} %collective-permute-done.2), channel_id=1, source_target_pairs={{0,1},{1,2},{2,3},{3,4},{4,5},{5,6},{6,7},{7,0},{8,9},{9,10},{10,1... | collective-permute-start | bytes 12582920 | tf_op jit(solution)/shard_map/ppermute | solution.py:16
  1789.1 185.2 %collective-permute-start.6 = (bf16[4,256,2048]{2,1,0:T(8,128)(2,1)}, bf16[4,256,2048]{2,1,0:T(8,128)(2,1)}, u32[]{:S(2)}, u32[]{:S(2)}) collective-permute-start(bf16[4,256,2048]{2,1,0:T(8,128)(2,1)} %collective-permute-done.5), channel_id=1, source_target_pairs={{0,7},{1,0},{2,1},{3,2},{4,3},{5,4},{6,5},{7,6},{8,15},{9,8},{10,9... | collective-permute-start | bytes 12582920 | tf_op jit(solution)/shard_map/ppermute | solution.py:18
  1814.6 5.0 copy-start.21
  1819.6 3.7 copy-start.2
  2171.3 190.1 %all-to-all-start.1 = ((bf16[4,1024,2048]{2,0,1:T(4,128)(2,1)}), bf16[4,1024,2048]{2,0,1:T(4,128)(2,1)}, u32[]{:S(2)}, u32[]{:S(2)}) async-start(bf16[4,1024,2048]{2,0,1:T(4,128)(2,1)} %copy.196), calls=%async_computation.1 | async-start | bytes 33554432 | tf_op jit(solution)/shard_map/all_to_all | solution.py:143
  2243.8 125.0 %copy-start.61 = (s32[2048,1]{0,1:T(1,128)S(1)}, s32[2048,1]{0,1:T(1,128)}, u32[]{:S(2)}) copy-start(s32[2048,1]{0,1:T(1,128)} %copy-done.60) | copy-start | bytes 24580
  2361.3 190.5 %all-to-all-start.3 = ((bf16[4,1024,2048]{2,0,1:T(4,128)(2,1)}), bf16[4,1024,2048]{2,0,1:T(4,128)(2,1)}, u32[]{:S(2)}, u32[]{:S(2)}) async-start(bf16[4,1024,2048]{2,0,1:T(4,128)(2,1)} %copy.202), calls=%async_computation.3 | async-start | bytes 33554432 | tf_op jit(solution)/shard_map/all_to_all | solution.py:185
  2368.8 483.3 %reduce-scatter.8.cloned.1.call-start = ((), (), s32[]{:S(2)}) async-start(), calls=%async_computation.14 | async-start | bytes 9437184 | tf_op jit(solution)/shard_map/reduce_scatter | solution.py:258
  2387.5 24.4 copy-start.12
  2387.5 24.4 copy-start.35
  2411.9 9.6 copy-start.44
  2411.9 9.6 copy-start.63
  2411.9 9.6 copy-start.67
  2411.9 9.6 copy-start.58
  2594.9 11.4 copy-start.4
  2594.9 11.4 copy-start.40
  2594.9 11.4 copy-start.56
  2594.9 11.4 copy-start.65
  2606.3 3.1 copy-start.29
  2606.3 3.1 copy-start.30
  2609.5 3.1 copy-start.23
  2618.2 640.8 %reduce-scatter.6.cloned.1.call-start = ((), (), s32[]{:S(2)}) async-start(), calls=%async_computation.13 | async-start | bytes 28311552 | tf_op jit(solution)/shard_map/reduce_scatter | solution.py:255
  2626.1 4.1 copy-start.1
  2633.4 2.2 copy-start.7
  2633.4 2.2 copy-start.41
  2633.4 2.2 copy-start.48
  2635.6 3.0 copy-start.14
  2656.2 659.6 %reduce-scatter.10.cloned.1.call-start = ((), (), s32[]{:S(2)}) async-start(), calls=%async_computation.15 | async-start | bytes 73728 | tf_op jit(solution)/shard_map/reduce_scatter | solution.py:261
  2658.4 944.5 %reduce-scatter.14.cloned.1.call-start = ((), (), s32[]{:S(2)}) async-start(), calls=%async_computation.17 | async-start | bytes 18874368 | tf_op jit(solution)/shard_map/reduce_scatter | solution.py:192
  2685.3 1004.7 %all-reduce.4.cloned.1.call-start = ((), (), s32[]{:S(2)}) async-start(), calls=%async_computation.18 | async-start | bytes 8388608 | tf_op jit(solution)/shard_map/psum | solution.py:266
  3259.0 978.3 %reduce-scatter.12.cloned.1.call-start = ((), (), s32[]{:S(2)}) async-start(), calls=%async_computation.16 | async-start | bytes 37748736 | tf_op jit(solution)/shard_map/reduce_scatter | solution.py:189
  3322.4 14.9 copy-start.59
  3322.4 14.9 copy-start.72
  3322.4 14.9 copy-start.73
  3322.4 58.7 %copy-start.10 = (f32[256,2048]{1,0:T(8,128)S(1)}, f32[256,2048]{1,0:T(8,128)}, u32[]{:S(2)}) copy-start(f32[256,2048]{1,0:T(8,128)} %copy-done.8) | copy-start | bytes 6291460
  3690.0 5.4 copy-start.36
  (31 other events, 44.4 us)
Sparse Core Ops, SparseCore 0:
  9.5 483.1 all-gather.4
  494.8 124.8 all-gather.6
  622.0 443.4 all-gather.8
  1066.8 992.2 all-gather.10
  2618.3 233.6 reduce-scatter.7
  2856.3 402.6 reduce-scatter.5
  3263.0 52.8 reduce-scatter.9
  3320.1 282.6 reduce-scatter.13
  3605.3 84.6 all-reduce.3
  3694.0 543.1 reduce-scatter.11
